TPU v7x, 256 devices: a whole 4x4x8 slice. The times are simulated.
256 devices in a mesh: row: 16 (over x_hi, z), blk: 16 (over x_lo, y, core).
Axes of the slice: x: 4 (x_hi: 2, x_lo: 2; x = x_hi * 2 + x_lo), y: 4, z: 8, core: 2. Of those that a mesh axis runs over, the one named last changes fastest.
Arguments:
- source_table: bfloat16 [8192, 512], P('blk'), may hold values from -6 to 6
- target_table: bfloat16 [131072, 512], P(('row', 'blk')), may hold values from -6 to 6
- message_weight: bfloat16 [512, 512], replicated, may hold values from -0.25 to 0.25
- self_weight: bfloat16 [512, 512], replicated, may hold values from -0.25 to 0.25
- tile_lists: int32 [256, 16], P(('row', 'blk')), may hold values from 0 to 15, each once within a row
- key_offsets: int32 [131072, 16], P(('row', 'blk')), may hold values from 0 to 511
- list_lengths: int32 [256], P(('row', 'blk')), may hold values from 1 to 16, 2048 in all
- cotangent: bfloat16 [131072, 512], P(('row', 'blk')), may hold values from -6 to 6
Outputs:
- updated: bfloat16 [131072, 512], P(('row', 'blk'))
- target_gradient: bfloat16 [131072, 512], P(('row', 'blk'))
- source_gradient: bfloat16 [8192, 512], P(('blk', 'row'))
- self_gradient: float32 [512, 512], replicated
- message_gradient: float32 [512, 512], replicated
Inputs may be any that keep to these rules, and one draw needn't show every extreme that they name: Each row of tile_lists names every one of the 16 source tiles once. A target tile uses the first list_lengths entries of its row of tile_lists.
All inputs are finite; a program needn't handle non-finite values. No bound on the sum of `list_lengths` on one device may be relied on, other than what follows from the above.
Results may differ from a plain program's by a relative error of at most 0.0058.
Values may be sent and summed in bfloat16 or wider, within the bound.
A program may use at most 64 MiB of HBM per device.

v0:
```python
import jax
import jax.numpy as jnp
from jax import lax
from jax.sharding import PartitionSpec as P


def slot_table(lists):
    slot_count = lists.shape[1]
    slot_ids = lax.iota(jnp.int32, slot_count)
    matches = lists[:, :, None] == slot_ids[None, None, :]
    return jnp.sum(jnp.where(matches, slot_ids[None, :, None], 0), axis=1)


def tile_patterns(offset_tiles, slot_column, lengths, tile_rows):
    slot_count = offset_tiles.shape[2]
    chosen_slot = lax.iota(jnp.int32, slot_count)[None, None, :] == slot_column[:, None, None]
    chosen = jnp.sum(jnp.where(chosen_slot, offset_tiles, 0), axis=2)
    used = slot_column < lengths
    positions = lax.iota(jnp.int32, tile_rows)
    pattern = (chosen[:, :, None] == positions[None, None, :]) & used[:, None, None]
    return pattern.astype(jnp.bfloat16)


def local(
    source_table,
    target_table,
    message_weight,
    self_weight,
    tile_lists,
    key_offsets,
    list_lengths,
    cotangent,
):
    tile_rows = target_table.shape[0] // tile_lists.shape[0]
    tiles_here = tile_lists.shape[0]
    slot_count = tile_lists.shape[1]
    width = target_table.shape[1]
    block_rows = source_table.shape[0]
    row_devices = lax.axis_size("row")
    share_rows = block_rows // row_devices
    own_rows = lax.dynamic_slice_in_dim(
        source_table, lax.axis_index("row") * share_rows, share_rows, 0
    )
    projected = jnp.dot(source_table, message_weight, preferred_element_type=jnp.float32).astype(
        jnp.bfloat16
    )
    inverse_tile = 1.0 / list_lengths.astype(jnp.float32)
    slot_of = slot_table(tile_lists)
    offset_tiles = key_offsets.reshape(tiles_here, tile_rows, slot_count)
    start_sum = jnp.zeros((target_table.shape[0], width), jnp.float32)
    pieces = lax.all_gather(projected, "blk", axis=0, tiled=True)
    piece_tiles = pieces.shape[0] // tile_rows

    def gather_visit(local_tile, running):
        source_tile = lax.dynamic_slice_in_dim(pieces, local_tile * tile_rows, tile_rows, 0)
        slot_column = lax.dynamic_index_in_dim(slot_of, local_tile, 1, keepdims=False)
        pattern = tile_patterns(offset_tiles, slot_column, list_lengths, tile_rows)
        added = jnp.einsum("trc,cw->trw", pattern, source_tile, preferred_element_type=jnp.float32)
        return running + added.reshape(running.shape)

    gathered = lax.fori_loop(0, piece_tiles, gather_visit, start_sum)
    inverse_row = jnp.repeat(inverse_tile, tile_rows)[:, None]
    preact = (
        jnp.dot(target_table, self_weight, preferred_element_type=jnp.float32)
        + gathered * inverse_row
    )
    sigmoid_pre = jax.nn.sigmoid(preact)
    updated = (target_table.astype(jnp.float32) + preact * sigmoid_pre).astype(jnp.bfloat16)
    upstream = cotangent.astype(jnp.float32)
    grad_pre = (upstream * sigmoid_pre * (1.0 + preact * (1.0 - sigmoid_pre))).astype(jnp.bfloat16)
    target_gradient = (
        upstream + jnp.dot(grad_pre, self_weight.T, preferred_element_type=jnp.float32)
    ).astype(jnp.bfloat16)
    grad_tiles = grad_pre.reshape(tiles_here, tile_rows, width)

    def tile_terms(slot_column, offsets, lengths, inverses, grads):
        pattern = tile_patterns(offsets, slot_column, lengths, tile_rows)
        terms = jnp.einsum("trc,trw->tcw", pattern, grads, preferred_element_type=jnp.float32)
        return jnp.sum(terms * inverses[:, None, None], axis=0)

    def partial_visit(local_tile, running):
        slot_column = lax.dynamic_index_in_dim(slot_of, local_tile, 1, keepdims=False)
        term = tile_terms(slot_column, offset_tiles, list_lengths, inverse_tile, grad_tiles)
        return lax.dynamic_update_slice_in_dim(running, term, local_tile * tile_rows, 0)

    block_sum = lax.psum_scatter(
        lax.fori_loop(
            0,
            block_rows * lax.axis_size("blk") // tile_rows,
            partial_visit,
            jnp.zeros((block_rows * lax.axis_size("blk"), width), jnp.float32),
        ),
        "blk",
        scatter_dimension=0,
        tiled=True,
    )
    source_sum = lax.psum_scatter(block_sum, "row", scatter_dimension=0, tiled=True)
    source_grad_rounded = source_sum.astype(jnp.bfloat16)
    source_gradient = jnp.dot(
        source_grad_rounded, message_weight.T, preferred_element_type=jnp.float32
    ).astype(jnp.bfloat16)
    self_partial = jnp.dot(target_table.T, grad_pre, preferred_element_type=jnp.float32)
    message_partial = jnp.dot(own_rows.T, source_grad_rounded, preferred_element_type=jnp.float32)
    self_total, message_total = lax.psum((self_partial, message_partial), ("row", "blk"))
    target_total = target_table.shape[0] * row_devices * lax.axis_size("blk")
    source_total = block_rows * lax.axis_size("blk")
    self_gradient = self_total * target_total ** (-0.5)
    message_gradient = message_total * source_total ** (-0.5)
    return (updated, target_gradient, source_gradient, self_gradient, message_gradient)


def solution(mesh):
    placed = (
        P("blk", None),
        P(("row", "blk"), None),
        P(),
        P(),
        P(("row", "blk"), None),
        P(("row", "blk"), None),
        P(("row", "blk")),
        P(("row", "blk"), None),
    )
    return jax.shard_map(
        local,
        mesh=mesh,
        in_specs=placed,
        out_specs=(
            P(("row", "blk"), None),
            P(("row", "blk"), None),
            P(("blk", "row"), None),
            P(),
            P(),
        ),
        check_vma=False,
    )
```

profile of v0, /device:TPU:2, one launch (start us, length us, event | category | flops | bytes accessed | tf_op | source)
XLA Modules:
  0.0 807.8 jit_solution(3190670035176118978)
XLA Ops:
  7.2 2.5 convolution_convert_fusion
  11.2 56.8 %all-gather.2.cloned.1.call-done = bf16[8192,512]{1,0:T(8,128)(2,1)} async-done(((bf16[512,512]{1,0:T(8,128)(2,1)}), bf16[8192,512]{1,0:T(8,128)(2,1)}) %all-gather.2.cloned.1.call-update) | async-done | bytes 8388624 | tf_op jit(solution)/shard_map/all_gather | solution.py:51
  68.0 80.6 %while.28 = (s32[]{:T(128)}, f32[512,512]{1,0:T(8,128)S(1)}, s32[1,16]{1,0:T(1,128)S(1)}, s32[1,512,16]{1,2,0:T(8,128)}, s32[1]{0:T(128)}, /*index=5*/bf16[8192,...) while((s32[]{:T(128)}, f32[512,512]{1,0:T(8,128)S(1)}, s32[1,16]{1,0:T(1,128)S(1)}, ...), condition=%wide.region_3.4_spmd.clone, body=%wide.region_1.3_spmd.clone.sunk | while | flops 269499936 | bytes 2659034 | solution.py:61
  71.4 1.6 convolution_add_fusion.4
  76.4 1.6 convolution_add_fusion.4
  81.5 1.6 convolution_add_fusion.4
  86.5 1.6 convolution_add_fusion.4
  91.6 1.6 convolution_add_fusion.4
  96.6 1.6 convolution_add_fusion.4
  101.6 1.6 convolution_add_fusion.4
  106.7 1.6 convolution_add_fusion.4
  111.7 1.6 convolution_add_fusion.4
  116.8 1.6 convolution_add_fusion.4
  121.8 1.6 convolution_add_fusion.4
  126.8 1.6 convolution_add_fusion.4
  131.9 1.6 convolution_add_fusion.4
  136.9 1.6 convolution_add_fusion.4
  142.0 1.6 convolution_add_fusion.4
  147.0 1.6 convolution_add_fusion.4
  148.7 3.0 fusion.15
  151.7 7.9 broadcast_in_dim.94
  159.6 67.2 %while.27 = (s32[]{:T(128)}, f32[8192,512]{1,0:T(8,128)}, s32[1,16]{1,0:T(1,128)S(1)}, s32[1,512,16]{1,2,0:T(8,128)S(1)}, s32[1]{0:T(128)}, /*index=5*/bf16[1,51...) while((s32[]{:T(128)}, f32[8192,512]{1,0:T(8,128)}, ...), condition=%wide.region_6.7_spmd, body=%wide.region_4.6_spmd.sunk | while | flops 269237792 | bytes 1610968 | solution.py:87
  166.4 1.6 fusion.37
  183.2 1.6 fusion.37
  195.8 1.6 fusion.37
  212.6 1.6 fusion.37
  226.8 101.1 %reduce-scatter.3.cloned.1.call-done = f32[512,512]{1,0:T(8,128)} async-done(((f32[8192,512]{1,0:T(8,128)}), f32[512,512]{1,0:T(8,128)}) %reduce-scatter.3.cloned.1.call-update) | async-done | bytes 1048592 | tf_op jit(solution)/shard_map/reduce_scatter | solution.py:86
  329.4 200.2 %reduce-scatter.5.cloned.1.call-done = f32[32,512]{1,0:T(8,128)} async-done(((f32[512,512]{1,0:T(8,128)}), f32[32,512]{1,0:T(8,128)}) %reduce-scatter.5.cloned.1.call-update) | async-done | bytes 65552 | tf_op jit(solution)/shard_map/reduce_scatter | solution.py:97
  529.6 2.1 fusion.16
  533.1 1.7 convolution_convert_fusion.1
  534.8 261.5 %all-reduce.3.cloned.1.call-done = (f32[512,512]{0,1:T(8,128)}, f32[512,512]{1,0:T(8,128)}) async-done(((f32[512,512]{0,1:T(8,128)}, f32[512,512]{1,0:T(8,128)}), (f32[512,512]{0,1:T(8,128)}, f32[512,512]{1,0:T(8,128)})) %all-reduce.3.cloned.1.call-update) | async-done | bytes 2097168 | tf_op jit(solution)/shard_map/psum | solution.py:104
  799.0 2.3 broadcast_multiply_fusion
  (132 shorter events, 79.4 us)
Async XLA Ops:
  7.2 141.5 %copy-start = (bf16[512,512]{1,0:T(8,128)(2,1)S(1)}, bf16[512,512]{1,0:T(8,128)(2,1)}, u32[]{:S(2)}) copy-start(bf16[512,512]{1,0:T(8,128)(2,1)} %param.15) | copy-start | bytes 1572868
  7.2 60.8 %all-gather.2.cloned.1.call-start = ((), (), s32[]{:S(2)}) async-start(), calls=%async_computation.2 | async-start | bytes 8912896 | tf_op jit(solution)/shard_map/all_gather | solution.py:51
  9.7 318.2 %reduce-scatter.3.cloned.1.call-start = ((), (), s32[]{:S(2)}) async-start(), calls=%async_computation.3 | async-start | bytes 17825792 | tf_op jit(solution)/shard_map/reduce_scatter | solution.py:86
  148.6 10.9 %copy-start.1 = (s32[1,512,16]{1,2,0:T(8,128)S(1)}, s32[1,512,16]{1,2,0:T(8,128)}, u32[]{:S(2)}) copy-start(s32[1,512,16]{1,2,0:T(8,128)} %get-tuple-element.461) | copy-start | bytes 98308
  159.6 168.4 %copy-start.3 = (bf16[512,512]{1,0:T(8,128)(2,1)S(1)}, bf16[512,512]{1,0:T(8,128)(2,1)}, u32[]{:S(2)}) copy-start(bf16[512,512]{1,0:T(8,128)(2,1)} %param.13) | copy-start | bytes 1572868
  159.6 372.2 %copy-start.4 = (bf16[512,512]{1,0:T(8,128)(2,1)S(1)}, bf16[512,512]{1,0:T(8,128)(2,1)}, u32[]{:S(2)}) copy-start(bf16[512,512]{1,0:T(8,128)(2,1)} %param.19) | copy-start | bytes 1572868
  159.6 373.5 %copy-start.2 = (bf16[512,512]{1,0:T(8,128)(2,1)S(1)}, bf16[512,512]{1,0:T(8,128)(2,1)}, u32[]{:S(2)}) copy-start(bf16[512,512]{1,0:T(8,128)(2,1)} %param.14) | copy-start | bytes 1572868
  226.8 302.9 %reduce-scatter.5.cloned.1.call-start = ((), (), s32[]{:S(2)}) async-start(), calls=%async_computation.4 | async-start | bytes 1114112 | tf_op jit(solution)/shard_map/reduce_scatter | solution.py:97
  327.9 468.4 %all-reduce.3.cloned.1.call-start = ((), (), s32[]{:S(2)}) async-start(), calls=%async_computation.5 | async-start | bytes 4194304 | tf_op jit(solution)/shard_map/psum | solution.py:104
Sparse Core Ops, SparseCore 0:
  10.4 57.5 all-gather.1
  226.9 100.9 reduce-scatter.2
  331.7 197.8 reduce-scatter.4
  535.6 260.6 all-reduce.2
where the time goes:
time: 811 us; the launch traced here: 808 us
  waiting for transfers between devices  620 us (76%)
  matrix products  63 us (8%)
  loops' own time  42.4 us (5%)
  other arithmetic  40.2 us (5%)
  local copies, waits for them, and re-layouts  27.9 us (3%)
  between operations  14.5 us (2%)
    psum x1, waiting for transfers between devices, local(): lax.psum((self_partial, message_partial), ('row', 'blk'))  262 us
    reduce_scatter x1, waiting for transfers between devices, local(): lax.psum_scatter(block_sum, 'row', scatter_dimension=0, tiled=True)  200 us
    reduce_scatter x1, waiting for transfers between devices, local(): lax.psum_scatter(lax.fori_loop(0, block_rows * lax.axis_size('blk') // ti...  101 us
    all_gather x1, waiting for transfers between devices, local(): pieces = lax.all_gather(projected, 'blk', axis=0, tiled=True)  56.8 us
    dot_general x16, matrix products, gather_visit(): jnp.einsum('trc,cw->trw', pattern, source_tile, preferred_element_type=jn...  25.9 us
    dot_general x16, matrix products, tile_terms(): jnp.einsum('trc,trw->tcw', pattern, grads, preferred_element_type=jnp.flo...  25.1 us
    another operation x1, loops' own time, local(): gathered = lax.fori_loop(0, piece_tiles, gather_visit, start_sum)  21.4 us
    another operation x1, loops' own time, local(): lax.fori_loop(0, block_rows * lax.axis_size('blk') // tile_rows, partial_...  21 us
  transfers between devices with their start and end apart: 4, of which 4 were waited for; matrix products, arithmetic and copies ran while one was open for 1% of the time, Pallas kernels for 0%

commit v1 on v0

--- a/solution.py
+++ b/solution.py
@@ -48,7 +48,9 @@
     slot_of = slot_table(tile_lists)
     offset_tiles = key_offsets.reshape(tiles_here, tile_rows, slot_count)
     start_sum = jnp.zeros((target_table.shape[0], width), jnp.float32)
-    pieces = lax.all_gather(projected, "blk", axis=0, tiled=True)
+    pieces = jnp.concatenate(
+        lax.all_to_all(jnp.stack([projected] * lax.axis_size("blk")), "blk", 0, 0), axis=0
+    )
     piece_tiles = pieces.shape[0] // tile_rows
 
     def gather_visit(local_tile, running):

time: 811 us -> 877 us (1.081)
  waiting for transfers between devices: 620 us -> 691 us
  other arithmetic: 40.2 us -> 27.4 us
    all_to_all x0 -> x1, waiting for transfers between devices: none -> 120 us  [local(): lax.all_to_all(jnp.stack([projected] * lax.axis_size('blk')), 'blk', 0, 0)]
    all_gather x1 -> x0, waiting for transfers between devices: 56.8 us -> none  [local(): pieces = lax.all_gather(projected, 'blk', axis=0, tiled=True)]
    reduce_sum x32, other arithmetic: 15 us -> 2.91 us  [tile_patterns(): chosen = jnp.sum(jnp.where(chosen_slot, offset_tiles, 0), axis=2)]
where the time goes in v1:
time: 877 us; the launch traced here: 875 us
  waiting for transfers between devices  691 us (79%)
  matrix products  60.9 us (7%)
  loops' own time  42.4 us (5%)
  local copies, waits for them, and re-layouts  31.9 us (4%)
  other arithmetic  27.4 us (3%)
  between operations  14.5 us (2%)
    psum x1, waiting for transfers between devices, local(): lax.psum((self_partial, message_partial), ('row', 'blk'))  262 us
    reduce_scatter x1, waiting for transfers between devices, local(): lax.psum_scatter(block_sum, 'row', scatter_dimension=0, tiled=True)  200 us
    all_to_all x1, waiting for transfers between devices, local(): lax.all_to_all(jnp.stack([projected] * lax.axis_size('blk')), 'blk', 0, 0)  120 us
    reduce_scatter x1, waiting for transfers between devices, local(): lax.psum_scatter(lax.fori_loop(0, block_rows * lax.axis_size('blk') // ti...  109 us
    dot_general x16, matrix products, gather_visit(): jnp.einsum('trc,cw->trw', pattern, source_tile, preferred_element_type=jn...  25.9 us
    dot_general x16, matrix products, tile_terms(): jnp.einsum('trc,trw->tcw', pattern, grads, preferred_element_type=jnp.flo...  25.1 us
    another operation x1, loops' own time, local(): gathered = lax.fori_loop(0, piece_tiles, gather_visit, start_sum)  21.4 us
    another operation x1, loops' own time, local(): lax.fori_loop(0, block_rows * lax.axis_size('blk') // tile_rows, partial_...  20.9 us
  transfers between devices with their start and end apart: 4, of which 4 were waited for; matrix products, arithmetic and copies ran while one was open for 1% of the time, Pallas kernels for 0%

profile of v1, /device:TPU:2, one launch (start us, length us, event | category | flops | bytes accessed | tf_op | source)
XLA Modules:
  0.0 874.8 jit_solution(6938814341370827293)
XLA Ops:
  7.2 1.7 convolution_convert_fusion
  8.9 4.0 stack.2
  12.9 6.9 all-to-all-start
  20.7 120.3 %all-to-all-done = bf16[16,512,512]{2,1,0:T(8,128)(2,1)} async-done(((bf16[16,512,512]{2,1,0:T(8,128)(2,1)}), bf16[16,512,512]{2,1,0:T(8,128)(2,1)}, u32[]{:S(2)}, u32[]{:S(2)}) %all-to-all-start) | async-done | bytes 8388640 | tf_op jit(solution)/shard_map/all_to_all | solution.py:52
  141.0 68.5 %while.28 = (s32[]{:T(128)}, f32[512,512]{1,0:T(8,128)S(1)}, s32[1,16]{1,0:T(1,128)S(1)}, s32[1,512,16]{1,2,0:T(8,128)S(1)}, s32[1]{0:T(128)}, /*index=5*/bf16[8...) while((s32[]{:T(128)}, f32[512,512]{1,0:T(8,128)S(1)}, s32[1,16]{1,0:T(1,128)S(1)}, ...), condition=%wide.region_3.4_spmd.clone, body=%wide.region_1.3_spmd.clone.sunk | while | flops 269499936 | bytes 2659034 | solution.py:63
  143.6 1.6 convolution_add_fusion.4
  147.9 1.6 convolution_add_fusion.4
  152.2 1.6 convolution_add_fusion.4
  156.5 1.6 convolution_add_fusion.4
  160.8 1.6 convolution_add_fusion.4
  165.0 1.6 convolution_add_fusion.4
  169.3 1.6 convolution_add_fusion.4
  173.6 1.6 convolution_add_fusion.4
  177.9 1.6 convolution_add_fusion.4
  182.2 1.6 convolution_add_fusion.4
  186.5 1.6 convolution_add_fusion.4
  190.7 1.6 convolution_add_fusion.4
  195.0 1.6 convolution_add_fusion.4
  199.3 1.6 convolution_add_fusion.4
  203.6 1.6 convolution_add_fusion.4
  207.9 1.6 convolution_add_fusion.4
  209.5 1.7 fusion.15
  211.2 7.9 broadcast_in_dim.94
  219.1 67.1 %while.27 = (s32[]{:T(128)}, f32[8192,512]{1,0:T(8,128)}, s32[1,16]{1,0:T(1,128)S(1)}, s32[1,512,16]{1,2,0:T(8,128)S(1)}, s32[1]{0:T(128)}, /*index=5*/bf16[1,51...) while((s32[]{:T(128)}, f32[8192,512]{1,0:T(8,128)}, ...), condition=%wide.region_6.7_spmd, body=%wide.region_4.6_spmd.sunk | while | flops 269237792 | bytes 1610968 | solution.py:89
  255.3 1.6 fusion.37
  272.1 1.6 fusion.37
  286.3 108.5 %reduce-scatter.3.cloned.1.call-done = f32[512,512]{1,0:T(8,128)} async-done(((f32[8192,512]{1,0:T(8,128)}), f32[512,512]{1,0:T(8,128)}) %reduce-scatter.3.cloned.1.call-update) | async-done | bytes 1048592 | tf_op jit(solution)/shard_map/reduce_scatter | solution.py:88
  396.3 200.2 %reduce-scatter.5.cloned.1.call-done = f32[32,512]{1,0:T(8,128)} async-done(((f32[512,512]{1,0:T(8,128)}), f32[32,512]{1,0:T(8,128)}) %reduce-scatter.5.cloned.1.call-update) | async-done | bytes 65552 | tf_op jit(solution)/shard_map/reduce_scatter | solution.py:99
  596.5 2.1 fusion.16
  600.0 1.7 convolution_convert_fusion.1
  601.7 261.6 %all-reduce.3.cloned.1.call-done = (f32[512,512]{0,1:T(8,128)}, f32[512,512]{1,0:T(8,128)}) async-done(((f32[512,512]{0,1:T(8,128)}, f32[512,512]{1,0:T(8,128)}), (f32[512,512]{0,1:T(8,128)}, f32[512,512]{1,0:T(8,128)})) %all-reduce.3.cloned.1.call-update) | async-done | bytes 2097168 | tf_op jit(solution)/shard_map/psum | solution.py:106
  865.9 2.3 broadcast_multiply_fusion
  (134 shorter events, 69.8 us)
Async XLA Ops:
  7.2 202.4 %copy-start = (bf16[512,512]{1,0:T(8,128)(2,1)S(1)}, bf16[512,512]{1,0:T(8,128)(2,1)}, u32[]{:S(2)}) copy-start(bf16[512,512]{1,0:T(8,128)(2,1)} %param.15) | copy-start | bytes 1572868
  7.2 13.4 %copy-start.5 = (s32[1,16]{1,0:T(1,128)S(1)}, s32[1,16]{1,0:T(1,128)}, u32[]{:S(2)}) copy-start(s32[1,16]{1,0:T(1,128)} %param.16) | copy-start | bytes 196
  7.2 133.8 %copy-start.1 = (s32[512,16]{0,1:T(8,128)S(1)}, s32[512,16]{0,1:T(8,128)}, u32[]{:S(2)}) copy-start(s32[512,16]{0,1:T(8,128)} %param.17) | copy-start | bytes 98308
  12.9 196.6 %copy-start.3 = (bf16[512,512]{1,0:T(8,128)(2,1)S(1)}, bf16[512,512]{1,0:T(8,128)(2,1)}, u32[]{:S(2)}) copy-start(bf16[512,512]{1,0:T(8,128)(2,1)} %param.13) | copy-start | bytes 1572868
  12.9 196.6 %copy-start.4 = (bf16[512,512]{1,0:T(8,128)(2,1)S(1)}, bf16[512,512]{1,0:T(8,128)(2,1)}, u32[]{:S(2)}) copy-start(bf16[512,512]{1,0:T(8,128)(2,1)} %param.19) | copy-start | bytes 1572868
  12.9 128.1 %all-to-all-start = ((bf16[16,512,512]{2,1,0:T(8,128)(2,1)}), bf16[16,512,512]{2,1,0:T(8,128)(2,1)}, u32[]{:S(2)}, u32[]{:S(2)}) async-start(bf16[16,512,512]{2,1,0:T(8,128)(2,1)} %stack.2), calls=%async_computation | async-start | bytes 16777216 | tf_op jit(solution)/shard_map/all_to_all | solution.py:52
  19.9 374.9 %reduce-scatter.3.cloned.1.call-start = ((), (), s32[]{:S(2)}) async-start(), calls=%async_computation.3 | async-start | bytes 17825792 | tf_op jit(solution)/shard_map/reduce_scatter | solution.py:88
  219.1 380.9 %copy-start.2 = (bf16[512,512]{1,0:T(8,128)(2,1)S(1)}, bf16[512,512]{1,0:T(8,128)(2,1)}, u32[]{:S(2)}) copy-start(bf16[512,512]{1,0:T(8,128)(2,1)} %param.14) | copy-start | bytes 1572868
  286.2 310.3 %reduce-scatter.5.cloned.1.call-start = ((), (), s32[]{:S(2)}) async-start(), calls=%async_computation.4 | async-start | bytes 1114112 | tf_op jit(solution)/shard_map/reduce_scatter | solution.py:99
  394.8 468.5 %all-reduce.3.cloned.1.call-start = ((), (), s32[]{:S(2)}) async-start(), calls=%async_computation.5 | async-start | bytes 4194304 | tf_op jit(solution)/shard_map/psum | solution.py:106
Sparse Core Ops, SparseCore 0:
  286.4 108.3 reduce-scatter.2
  398.6 197.8 reduce-scatter.4
  602.7 260.5 all-reduce.2
